TPU v7x, 32 devices: a whole 2x2x4 slice. The times are simulated.
32 devices in a mesh: batch: 2 (over x), rows: 16 (over z, y, core).
Axes of the slice: x: 2, y: 2, z: 4, core: 2. Of those that a mesh axis runs over, the one named last changes fastest.
Arguments:
- layer_input: bfloat16 [2, 64, 64, 2048], P('batch', 'rows'), may hold values from -6 to 6
- pre_activation: bfloat16 [2, 64, 64, 2048], P('batch', 'rows'), may hold values from -6 to 6
- cotangent: bfloat16 [2, 64, 64, 2048], P('batch', 'rows'), may hold values from -6 to 6
- weight: bfloat16 [64, 64], replicated, may hold values from -0.75 to 0.75
- spectral: bfloat16 [2304, 64, 128], P('rows'), may hold values from -6 to 6
- slab_ids: int32 [2, 32], P('batch'), may hold values from 0 to 2047, as said below
- extents: int32 [2, 32], P('batch'), may hold values from 1 to 2048, as said below
Outputs:
- grad_input: bfloat16 [2, 64, 64, 2048], P('batch', 'rows')
- grad_spectral: float32 [2304, 64, 128], P('rows')
- grad_weight: float32 [64, 64], replicated
Inputs may be any that keep to these rules, and one draw needn't show every extreme that they name: `slab_ids`: within a sample the 32 slab numbers are distinct and include 0 and 2047; slots 2 k to 2 k + 1 are stored on index k of rows. `extents`: A slot's extent counts its slab's live columns from column 0.
All inputs are finite; a program needn't handle non-finite values.
Results may differ from a plain program's by a relative error of at most 0.0085.
Values may be sent and summed in bfloat16 or wider, within the bound.
No kernel may reach another device: no remote copies, remote signals or barrier semaphores. Data moves between devices by JAX's collectives and lax.ppermute only.
A program may use at most 128 MiB of HBM per device.

v0:
```python
import math
import jax
import jax.numpy as jnp
from jax import lax
from jax.sharding import PartitionSpec as P

PA = 48
SLAB = 2
NR = 4096
MODES = 96


def column_table(column_count, freq_count):
    column_index = jnp.arange(column_count, dtype=jnp.int32)
    freq_index = jnp.arange(freq_count, dtype=jnp.int32)
    phase = column_index[:, None] * freq_index[None, :] % column_count
    angle = phase.astype(jnp.float32) * (2.0 * math.pi / column_count)
    return jnp.concatenate([jnp.cos(angle), -jnp.sin(angle)], axis=1).astype(jnp.bfloat16)


def row_table(positions, row_total, freq_count):
    freq_index = jnp.arange(freq_count, dtype=jnp.int32) - freq_count // 2
    phase = jnp.mod(freq_index[:, None] * positions[None, :], row_total)
    angle = phase.astype(jnp.float32) * (2.0 * math.pi / row_total)
    return jnp.concatenate([jnp.cos(angle), jnp.sin(angle)], axis=0).astype(jnp.bfloat16)


def stored_positions(slab_list, slab_rows):
    offsets = jnp.tile(jnp.arange(slab_rows, dtype=jnp.int32), slab_list.shape[0])
    return jnp.repeat(slab_list, slab_rows) * slab_rows + offsets


def gelu_slope(values):
    return (
        0.5 * (1.0 + lax.erf(values * 0.7071067811865476))
        + values * jnp.exp(-0.5 * values * values) * 0.3989422804014327
    )


def row_combine(row_sums, scale):
    upper = row_sums[0]
    lower = row_sums[1]
    real_part = upper[:, :, 0] + lower[:, :, 1]
    imag_part = upper[:, :, 1] - lower[:, :, 0]
    return (jnp.stack([real_part, imag_part], axis=2) * scale).astype(jnp.bfloat16)


def to_blocks(spectra, half_modes):
    chans = spectra.shape[1]
    shaped = spectra.reshape(half_modes, 2, chans, 2, half_modes, 2)
    return shaped.transpose(2, 3, 1, 5, 0, 4).reshape(chans, 2, 2, 2, half_modes * half_modes)


def from_blocks(blocked, half_modes):
    chans = blocked.shape[0]
    shaped = blocked.reshape(chans, 2, 2, 2, half_modes, half_modes)
    return shaped.transpose(4, 2, 0, 1, 5, 3).reshape(2 * half_modes, chans, 2, 2 * half_modes)


def factor_pair(owned, chans):
    input_modes = owned[:chans]
    grad_out = owned[chans:]
    factor_left = input_modes.transpose(4, 0, 1, 2, 3).reshape(owned.shape[4], chans, 8)
    real_out = grad_out[:, 0]
    imag_out = grad_out[:, 1]
    first_half = jnp.stack([real_out, imag_out], axis=1)
    second_half = jnp.stack([imag_out, -real_out], axis=1)
    stacked = jnp.concatenate([first_half, second_half], axis=0)
    factor_right = stacked.transpose(4, 0, 1, 2, 3).reshape(owned.shape[4], 2 * chans, 8)
    return (factor_left, factor_right)


def modes_to_channels(grad_modes):
    blocks = grad_modes.shape[0]
    chans = grad_modes.shape[1]
    return grad_modes.reshape(blocks, chans, 2, 2, 2).transpose(1, 2, 3, 4, 0)


def row_adjoint(rowtab, grad_grid, scale):
    real_part = grad_grid[:, :, 0]
    imag_part = grad_grid[:, :, 1]
    upper = jnp.stack([real_part, imag_part], axis=2)
    lower = jnp.stack([-imag_part, real_part], axis=2)
    joined = jnp.concatenate([upper, lower], axis=0)
    summed = jnp.dot(
        rowtab.T, joined.reshape(joined.shape[0], -1), preferred_element_type=jnp.float32
    )
    return (summed * scale).astype(jnp.bfloat16)


def shards(layer_input, pre_activation, cotangent, weight, spectral, slab_ids, extents):
    batch_devices = lax.axis_size("batch")
    local_rows = layer_input.shape[1]
    channels = layer_input.shape[2]
    column_count = layer_input.shape[3]
    slab_list = slab_ids[0]
    active = slab_list.shape[0]
    slots = local_rows // SLAB
    scale = 1.0 / math.sqrt(NR * column_count)
    position = lax.axis_index("rows")
    own_extents = lax.dynamic_slice_in_dim(extents[0], position * slots, slots)
    column_index = jnp.arange(column_count, dtype=jnp.int32)
    alive = column_index[None, :] < jnp.repeat(own_extents, SLAB)[:, None]
    mask_half = alive.astype(jnp.bfloat16)
    mask_full = alive.astype(jnp.float32)
    masked_in = layer_input[0] * mask_half[:, None, :]
    grad_pre = (
        cotangent[0].astype(jnp.float32)
        * mask_full[:, None, :]
        * gelu_slope(pre_activation[0].astype(jnp.float32))
    ).astype(jnp.bfloat16)
    coltab = column_table(column_count, MODES)
    stacked = jnp.concatenate([masked_in, grad_pre], axis=1)
    colspec = jnp.dot(stacked.reshape(-1, column_count), coltab, preferred_element_type=jnp.float32)
    colspec = colspec.reshape(local_rows, 2 * channels, 2 * MODES).astype(jnp.bfloat16)
    gathered_rows = lax.all_to_all(colspec, "rows", split_axis=1, concat_axis=0, tiled=True)
    all_rows = gathered_rows.shape[0]
    owned_channels = gathered_rows.shape[1]
    rowtab = row_table(stored_positions(slab_list, SLAB), NR, MODES)
    row_sums = jnp.dot(
        rowtab, gathered_rows.reshape(all_rows, -1), preferred_element_type=jnp.float32
    )
    spectra = row_combine(row_sums.reshape(2, MODES, owned_channels, 2, MODES), scale)
    owned = lax.all_to_all(to_blocks(spectra, PA), "rows", split_axis=4, concat_axis=0, tiled=True)
    factor_left, factor_right = factor_pair(owned, channels)
    grad_modes = jnp.einsum(
        "bix,bxk->bik", spectral, factor_right, preferred_element_type=jnp.float32
    ).astype(jnp.bfloat16)
    own_grad = jnp.einsum(
        "bik,bxk->bix", factor_left, factor_right, preferred_element_type=jnp.float32
    )
    grad_spectral = lax.psum(own_grad, "batch")
    returned = lax.all_to_all(
        modes_to_channels(grad_modes), "rows", split_axis=0, concat_axis=4, tiled=True
    )
    rowback = row_adjoint(rowtab, from_blocks(returned, PA), scale)
    rowback = rowback.reshape(all_rows, -1, 2 * MODES)
    local_back = lax.all_to_all(rowback, "rows", split_axis=0, concat_axis=1, tiled=True)
    spatial = jnp.dot(
        local_back.reshape(-1, 2 * MODES), coltab.T, preferred_element_type=jnp.float32
    )
    spatial = spatial.reshape(local_rows, channels, column_count)
    row_weight = jnp.broadcast_to(weight, (local_rows, channels, channels))
    direct = jnp.einsum("rio,roc->ric", row_weight, grad_pre, preferred_element_type=jnp.float32)
    grad_input = ((spatial + direct) * mask_full[:, None, :]).astype(jnp.bfloat16)[None]
    row_partial = jnp.einsum(
        "ric,roc->rio", masked_in, grad_pre, preferred_element_type=jnp.float32
    )
    local_weight = jnp.sum(row_partial, axis=0)
    grad_weight = lax.psum(local_weight, ("batch", "rows"))
    grad_weight = grad_weight * (1.0 / math.sqrt(batch_devices * active * SLAB * column_count))
    return (grad_input, grad_spectral, grad_weight)


def solution(mesh):
    return jax.shard_map(
        shards,
        mesh=mesh,
        in_specs=(
            P("batch", "rows", None, None),
            P("batch", "rows", None, None),
            P("batch", "rows", None, None),
            P(),
            P("rows", None, None),
            P("batch", None),
            P("batch", None),
        ),
        out_specs=(P("batch", "rows", None, None), P("rows", None, None), P()),
        check_vma=False,
    )
```

profile of v0, /device:TPU:0, one launch (start us, length us, event | category | flops | bytes accessed | tf_op | source)
XLA Modules:
  0.0 304.3 jit_solution(13098841507869636662)
XLA Ops:
  7.2 3.9 %negate_convert_fusion = (bf16[2048,96]{0,1:T(8,128)(2,1)}, bf16[2048,96]{0,1:T(8,128)(2,1)}) fusion(), kind=kLoop, calls=%fused_computation.40 | loop fusion | flops 3342336 | bytes 786432 | tf_op jit(solution)/shard_map/convert.3
  18.4 7.5 %all-to-all-start = ((bf16[4,128,192]{2,0,1:T(4,128)(2,1)}), bf16[4,128,192]{2,0,1:T(4,128)(2,1)}, u32[]{:S(2)}, u32[]{:S(2)}) async-start(bf16[4,128,192]{2,0,1:T(4,128)(2,1)} %copy.52), calls=%async_computation | async-start | bytes 524288 | tf_op jit(solution)/shard_map/all_to_all | solution.py:116
  26.6 9.3 %all-to-all-done = bf16[4,128,192]{2,0,1:T(4,128)(2,1)} async-done(((bf16[4,128,192]{2,0,1:T(4,128)(2,1)}), bf16[4,128,192]{2,0,1:T(4,128)(2,1)}, u32[]{:S(2)}, u32[]{:S(2)}) %all-to-all-start) | async-done | bytes 196640 | tf_op jit(solution)/shard_map/all_to_all | solution.py:116
  41.9 3.0 squeeze.7
  44.8 3.1 %fusion.45 = (f32[96,8,1,96]{3,2,1,0:T(1,128)}, f32[96,8,1,96]{3,2,1,0:T(1,128)}) fusion(f32[96,8,2,96]{3,2,1,0:T(2,128)} %squeeze.7), kind=kLoop, calls=%fused_computation.82 | loop fusion | bytes 1179648 | tf_op jit(solution)/shard_map/slice | solution.py:43
  47.9 4.2 %copy.79 = f32[96,8,1,96]{1,3,0,2:T(8,128)} copy(f32[96,8,1,96]{3,2,1,0:T(1,128)} %get-tuple-element.10) | data formatting | bytes 589824
  52.1 3.0 squeeze.8
  55.1 2.9 fusion.44
  58.0 4.2 %copy.80 = f32[96,8,1,96]{1,3,0,2:T(8,128)} copy(f32[96,8,1,96]{3,2,1,0:T(1,128)} %get-tuple-element.8) | data formatting | bytes 589824
  62.2 6.9 %sub.9 = f32[96,8,1,96]{1,3,0,2:T(8,128)} subtract(f32[96,8,1,96]{1,3,0,2:T(8,128)} %copy.79, f32[96,8,1,96]{1,3,0,2:T(8,128)} %copy.80) | non-fusion elementwise | flops 73728 | bytes 884736 | tf_op jit(solution)/shard_map/sub | solution.py:44
  69.1 6.2 %copy.60 = f32[48,2,8,1,48,2]{4,2,5,3,1,0:T(8,128)} copy(f32[48,2,8,1,48,2]{2,5,4,1,0,3:T(2,128)} %bitcast.84) | data formatting | bytes 589824 | tf_op jit(solution)/shard_map/stack | solution.py:45
  75.3 4.2 %copy.77 = f32[96,8,1,96]{1,3,0,2:T(8,128)} copy(f32[96,8,1,96]{3,2,1,0:T(1,128)} %get-tuple-element.9) | data formatting | bytes 589824
  79.5 4.2 %copy.78 = f32[96,8,1,96]{1,3,0,2:T(8,128)} copy(f32[96,8,1,96]{3,2,1,0:T(1,128)} %get-tuple-element.7) | data formatting | bytes 589824
  83.7 6.9 %add.60 = f32[96,8,1,96]{1,3,0,2:T(8,128)} add(f32[96,8,1,96]{1,3,0,2:T(8,128)} %copy.77, f32[96,8,1,96]{1,3,0,2:T(8,128)} %copy.78) | non-fusion elementwise | flops 73728 | bytes 884736 | tf_op jit(solution)/shard_map/add | solution.py:43
  90.6 6.2 %copy.59 = f32[48,2,8,1,48,2]{4,2,5,3,1,0:T(8,128)} copy(f32[48,2,8,1,48,2]{2,5,4,1,0,3:T(2,128)} %bitcast.85) | data formatting | bytes 589824 | tf_op jit(solution)/shard_map/stack | solution.py:45
  99.3 9.3 %copy.74 = bf16[8,2,2,2,48,48]{0,3,2,1,5,4:T(2,128)(2,1)} copy(bf16[8,2,2,2,48,48]{5,0,3,1,2,4:T(8,128)(2,1)} %fusion.24) | data formatting | bytes 589824 | tf_op jit(solution)/shard_map/reshape | solution.py:51
  108.6 7.0 %reshape.131 = bf16[16,2,4608]{2,1,0:T(2,128)(2,1)} reshape(bf16[2304,2,2,2,8]{4,3,2,1,0:T(2,128)(2,1)} %bitcast.87) | data formatting | bytes 589824
  115.6 14.7 %all_to_all.60 = bf16[16,2,4608]{2,1,0:T(2,128)(2,1)} all-to-all(bf16[16,2,4608]{2,1,0:T(2,128)(2,1)} %reshape.131), channel_id=1, replica_groups=mesh['batch'=2,'rows'=16] {'rows'}, dimensions={0} | all-to-all | bytes 589824 | tf_op jit(solution)/shard_map/all_to_all | solution.py:124
  130.3 7.4 %reshape.132 = bf16[2304,2,2,2,8]{4,3,2,1,0:T(2,128)(2,1)} reshape(bf16[16,2,4608]{2,1,0:T(2,128)(2,1)} %all_to_all.60) | data formatting | bytes 589824
  137.7 12.1 %copy.75 = bf16[8,2,2,2,16,144]{5,4,0,3,2,1:T(8,128)(2,1)} copy(bf16[8,2,2,2,16,144]{0,3,2,1,5,4:T(2,128)(2,1)} %bitcast.88) | data formatting | bytes 589824 | tf_op jit(solution)/shard_map/all_to_all | solution.py:124
  158.1 4.0 %fusion.48 = f32[144,64,128]{2,1,0:T(8,128)} fusion(bf16[144,64,8]{1,2,0:T(8,128)(2,1)} %bitcast.97, bf16[144,128,8]{1,2,0:T(8,128)(2,1)} %bitcast.91), kind=kOutput, calls=%fused_computation.85 | convolution fusion | flops 18874368 | bytes 5160960 | tf_op jit(solution)/shard_map/bik,bxk->bix/dot_general | solution.py:129
  162.1 3.0 convolution_convert_fusion
  167.1 4.2 %all-to-all-start.2 = ((bf16[64,2,2,2,144]{4,3,2,1,0:T(2,128)(2,1)}), bf16[64,2,2,2,144]{4,3,2,1,0:T(2,128)(2,1)}, u32[]{:S(2)}, u32[]{:S(2)}) async-start(bf16[64,2,2,2,144]{4,3,2,1,0:T(2,128)(2,1)} %bitcast.98), calls=%async_computation.2 | async-start | bytes 524288 | tf_op jit(solution)/shard_map/all_to_all | solution.py:133
  173.0 42.4 %psum.15 = f32[64,64]{1,0:T(8,128)} all-reduce(f32[64,64]{1,0:T(8,128)S(1)} %convolution_bitcast_fusion.1), channel_id=1, replica_groups=mesh['batch'=2,'rows'=16] {'batch','rows'}, use_global_device_ids=true, to_apply=%region_1.2 | all-reduce | flops 4096 | bytes 32768 | tf_op jit(solution)/shard_map/psum | solution.py:150
  219.3 13.9 %copy.69 = bf16[48,2,4,2,48,2]{2,5,4,3,1,0:T(2,128)(2,1)} copy(bf16[48,2,4,2,48,2]{4,0,5,1,3,2:T(8,128)(2,1)} %bitcast.89) | data formatting | bytes 294912 | tf_op jit(solution)/shard_map/transpose | solution.py:57
  233.2 8.4 %copy.68 = bf16[48,2,4,2,48,2]{5,4,3,2,1,0:T(8,128)(2,1)} copy(bf16[48,2,4,2,48,2]{4,0,5,1,3,2:T(8,128)(2,1)} %bitcast.90) | data formatting | bytes 294912 | tf_op jit(solution)/shard_map/transpose | solution.py:57
  244.5 3.1 %pad_maximum_fusion = bf16[96,4,2,96]{1,3,2,0:T(8,128)(2,1)} fusion(bf16[96,4,1,96]{1,3,2,0:T(8,128)(2,1)S(1)} %get-tuple-element.4, bf16[96,4,1,96]{1,3,2,0:T(8,128)(2,1)S(1)} %get-tuple-element.3), kind=kLoop, calls=%fused_computation | loop fusion | flops 73728 | bytes 294912 | tf_op jit(solution)/shard_map/stack | solution.py:83
  247.6 4.9 %copy.70 = bf16[96,4,2,96]{3,2,1,0:T(2,128)(2,1)} copy(bf16[96,4,2,96]{1,3,2,0:T(8,128)(2,1)} %pad_maximum_fusion) | data formatting | bytes 294912 | tf_op jit(solution)/shard_map/stack | solution.py:83
  253.7 17.1 %concatenate.27 = bf16[96,768]{1,0:T(8,128)(2,1)} reshape(bf16[48,2,4,2,48,2]{5,4,3,2,1,0:T(8,128)(2,1)} %copy.68) | data formatting | bytes 294912 | tf_op jit(solution)/shard_map/concatenate | solution.py:84
  274.2 5.3 %all-to-all-start.3 = ((bf16[64,4,192]{2,1,0:T(4,128)(2,1)}), bf16[64,4,192]{2,1,0:T(4,128)(2,1)S(1)}, u32[]{:S(2)}, u32[]{:S(2)}) async-start(bf16[64,4,192]{2,1,0:T(4,128)(2,1)} %reshape.125), calls=%async_computation.3 | async-start | bytes 262144 | tf_op jit(solution)/shard_map/all_to_all | solution.py:138
  281.0 6.5 %all-to-all-done.3 = bf16[64,4,192]{2,1,0:T(4,128)(2,1)S(1)} async-done(((bf16[64,4,192]{2,1,0:T(4,128)(2,1)}), bf16[64,4,192]{2,1,0:T(4,128)(2,1)S(1)}, u32[]{:S(2)}, u32[]{:S(2)}) %all-to-all-start.3) | async-done | bytes 98336 | tf_op jit(solution)/shard_map/all_to_all | solution.py:138
  292.2 5.2 %copy.90 = f32[144,64,128]{2,1,0:T(8,128)} copy(f32[144,64,128]{2,1,0:T(8,128)} %all-reduce.2.cloned.1.call-done) | data formatting | bytes 9437184
  (67 shorter events, 45.8 us)
Async XLA Ops:
  7.2 154.9 %copy-start = (bf16[144,64,128]{2,1,0:T(8,128)(2,1)S(1)}, bf16[144,64,128]{2,1,0:T(8,128)(2,1)}, u32[]{:S(2)}) copy-start(bf16[144,64,128]{2,1,0:T(8,128)(2,1)} %param.11) | copy-start | bytes 7077892
  11.9 1.6 copy-start.4
  11.9 1.9 copy-start.5
  12.0 2.9 copy-start.6
  13.5 1.4 copy-start.1
  13.5 1.4 copy-start.2
  13.5 1.6 copy-start.3
  15.1 11.1 %copy-start.11 = (s32[1,32]{1,0:T(1,128)S(1)}, s32[1,32]{1,0:T(1,128)}, u32[]{:S(2)}) copy-start(s32[1,32]{1,0:T(1,128)} %param.12) | copy-start | bytes 388
  18.4 17.5 %all-to-all-start = ((bf16[4,128,192]{2,0,1:T(4,128)(2,1)}), bf16[4,128,192]{2,0,1:T(4,128)(2,1)}, u32[]{:S(2)}, u32[]{:S(2)}) async-start(bf16[4,128,192]{2,0,1:T(4,128)(2,1)} %copy.52), calls=%async_computation | async-start | bytes 524288 | tf_op jit(solution)/shard_map/all_to_all | solution.py:116
  25.9 266.3 %all-reduce.2.cloned.1.call-start = ((), (), s32[]{:S(2)}) async-start(), calls=%async_computation.4 | async-start | bytes 9437184 | tf_op jit(solution)/shard_map/psum | solution.py:132
  26.6 15.2 %copy-start.8 = (bf16[96,64]{1,0:T(8,128)(2,1)}, bf16[96,64]{1,0:T(8,128)(2,1)S(1)}, u32[]{:S(2)}) copy-start(bf16[96,64]{1,0:T(8,128)(2,1)S(1)} %get-tuple-element.15) | copy-start | bytes 36868
  26.6 15.2 %copy-start.9 = (bf16[96,64]{1,0:T(8,128)(2,1)}, bf16[96,64]{1,0:T(8,128)(2,1)S(1)}, u32[]{:S(2)}) copy-start(bf16[96,64]{1,0:T(8,128)(2,1)S(1)} %get-tuple-element.16) | copy-start | bytes 36868
  167.1 48.3 %all-to-all-start.2 = ((bf16[64,2,2,2,144]{4,3,2,1,0:T(2,128)(2,1)}), bf16[64,2,2,2,144]{4,3,2,1,0:T(2,128)(2,1)}, u32[]{:S(2)}, u32[]{:S(2)}) async-start(bf16[64,2,2,2,144]{4,3,2,1,0:T(2,128)(2,1)} %bitcast.98), calls=%async_computation.2 | async-start | bytes 524288 | tf_op jit(solution)/shard_map/all_to_all | solution.py:133
  272.5 18.2 %copy-start.10 = (bf16[64,64]{1,0:T(8,128)(2,1)S(1)}, bf16[64,64]{1,0:T(8,128)(2,1)}, u32[]{:S(2)}) copy-start(bf16[64,64]{1,0:T(8,128)(2,1)} %param.10) | copy-start | bytes 24580
  274.2 13.2 %all-to-all-start.3 = ((bf16[64,4,192]{2,1,0:T(4,128)(2,1)}), bf16[64,4,192]{2,1,0:T(4,128)(2,1)S(1)}, u32[]{:S(2)}, u32[]{:S(2)}) async-start(bf16[64,4,192]{2,1,0:T(4,128)(2,1)} %reshape.125), calls=%async_computation.3 | async-start | bytes 262144 | tf_op jit(solution)/shard_map/all_to_all | solution.py:138
  289.2 1.6 copy-start.7
Sparse Core Ops, SparseCore 0:
  162.2 119.0 all-reduce.1
where the time goes:
time: 309 us; the launch traced here: 304 us
  local copies, waits for them, and re-layouts  152 us (49%)
  blocking collectives  57.2 us (19%)
  other arithmetic  31.5 us (10%)
  starting transfers between devices  17.2 us (6%)
  matrix products  16.2 us (5%)
  waiting for transfers between devices  15.9 us (5%)
  between operations  14.3 us (5%)
    psum x1, blocking collectives, shards(): grad_weight = lax.psum(local_weight, ('batch', 'rows'))  42.4 us
    unnamed x31, local copies, waits for them, and re-layouts  36.7 us
    transpose x2, local copies, waits for them, and re-layouts, from_blocks(): shaped.transpose(4, 2, 0, 1, 5, 3)  22.3 us
    concatenate x2, local copies, waits for them, and re-layouts, row_adjoint(): joined = jnp.concatenate([upper, lower], axis=0)  18.2 us
    all_to_all x1, blocking collectives, shards(): lax.all_to_all(to_blocks(spectra, PA), 'rows', split_axis=4, concat_axis=...  14.7 us
    another operation x2, local copies, waits for them, and re-layouts, row_combine(): jnp.stack([real_part, imag_part], axis=2) * scale  12.3 us
    all_to_all x1, local copies, waits for them, and re-layouts, shards(): lax.all_to_all(to_blocks(spectra, PA), 'rows', split_axis=4, concat_axis=...  12.1 us
    all_to_all x1, waiting for transfers between devices, shards(): lax.all_to_all(colspec, 'rows', split_axis=1, concat_axis=0, tiled=True)  9.32 us
  transfers between devices with their start and end apart: 4, of which 2 were waited for; matrix products, arithmetic and copies ran while one was open for 24% of the time, Pallas kernels for 0%

commit v1 on v0

--- a/solution.py
+++ b/solution.py
@@ -121,7 +121,15 @@
         rowtab, gathered_rows.reshape(all_rows, -1), preferred_element_type=jnp.float32
     )
     spectra = row_combine(row_sums.reshape(2, MODES, owned_channels, 2, MODES), scale)
-    owned = lax.all_to_all(to_blocks(spectra, PA), "rows", split_axis=4, concat_axis=0, tiled=True)
+    owned = jnp.concatenate(
+        lax.all_to_all(
+            jnp.stack(jnp.split(to_blocks(spectra, PA), lax.axis_size("rows"), axis=4)),
+            "rows",
+            0,
+            0,
+        ),
+        axis=0,
+    )
     factor_left, factor_right = factor_pair(owned, channels)
     grad_modes = jnp.einsum(
         "bix,bxk->bik", spectral, factor_right, preferred_element_type=jnp.float32

time: 309 us -> 291 us (0.942)
  local copies, waits for them, and re-layouts: 152 us -> 133 us
    all_to_all x1 -> x0, local copies, waits for them, and re-layouts: 12.1 us -> none  [shards(): lax.all_to_all(to_blocks(spectra, PA), 'rows', split_axis=4, concat_axis=...]
    reshape x1, local copies, waits for them, and re-layouts: 9.32 us -> 2.61 us  [to_blocks(): shaped.transpose(2, 3, 1, 5, 0, 4)]
    unnamed x31 -> x44, local copies, waits for them, and re-layouts: 36.7 us -> 35.3 us
  transfers between devices with their start and end apart: 4 -> 4, of which waited for: 2 -> 2; matrix products, arithmetic and copies ran while one was open for 24% -> 25% of each run, Pallas kernels for 0% -> 0%
where the time goes in v1:
time: 291 us; the launch traced here: 286 us
  local copies, waits for them, and re-layouts  133 us (46%)
  blocking collectives  59.3 us (20%)
  other arithmetic  30.6 us (11%)
  starting transfers between devices  17.5 us (6%)
  matrix products  16.2 us (6%)
  waiting for transfers between devices  15.9 us (5%)
  between operations  14.3 us (5%)
    psum x1, blocking collectives, shards(): grad_weight = lax.psum(local_weight, ('batch', 'rows'))  42.3 us
    unnamed x44, local copies, waits for them, and re-layouts  35.3 us
    transpose x2, local copies, waits for them, and re-layouts, from_blocks(): shaped.transpose(4, 2, 0, 1, 5, 3)  22.3 us
    concatenate x2, local copies, waits for them, and re-layouts, row_adjoint(): joined = jnp.concatenate([upper, lower], axis=0)  18.2 us
    all_to_all x1, blocking collectives, shards(): lax.all_to_all(jnp.stack(jnp.split(to_blocks(spectra, PA), lax.axis_size(...  16.9 us
    another operation x2, local copies, waits for them, and re-layouts, row_combine(): jnp.stack([real_part, imag_part], axis=2) * scale  12.3 us
    all_to_all x1, waiting for transfers between devices, shards(): lax.all_to_all(colspec, 'rows', split_axis=1, concat_axis=0, tiled=True)  9.32 us
    all_to_all x1, starting transfers between devices, shards(): lax.all_to_all(colspec, 'rows', split_axis=1, concat_axis=0, tiled=True)  7.46 us
  transfers between devices with their start and end apart: 4, of which 2 were waited for; matrix products, arithmetic and copies ran while one was open for 25% of the time, Pallas kernels for 0%

profile of v1, /device:TPU:0, one launch (start us, length us, event | category | flops | bytes accessed | tf_op | source)
XLA Modules:
  0.0 286.5 jit_solution(14743403533956134839)
XLA Ops:
  7.2 3.9 %negate_convert_fusion = (bf16[2048,96]{0,1:T(8,128)(2,1)}, bf16[2048,96]{0,1:T(8,128)(2,1)}) fusion(), kind=kLoop, calls=%fused_computation.40 | loop fusion | flops 3342336 | bytes 786432 | tf_op jit(solution)/shard_map/convert.3
  18.4 7.5 %all-to-all-start = ((bf16[4,128,192]{2,0,1:T(4,128)(2,1)}), bf16[4,128,192]{2,0,1:T(4,128)(2,1)}, u32[]{:S(2)}, u32[]{:S(2)}) async-start(bf16[4,128,192]{2,0,1:T(4,128)(2,1)} %copy.65), calls=%async_computation | async-start | bytes 524288 | tf_op jit(solution)/shard_map/all_to_all | solution.py:116
  26.6 9.3 %all-to-all-done = bf16[4,128,192]{2,0,1:T(4,128)(2,1)} async-done(((bf16[4,128,192]{2,0,1:T(4,128)(2,1)}), bf16[4,128,192]{2,0,1:T(4,128)(2,1)}, u32[]{:S(2)}, u32[]{:S(2)}) %all-to-all-start) | async-done | bytes 196640 | tf_op jit(solution)/shard_map/all_to_all | solution.py:116
  41.9 3.0 %squeeze.7 = f32[96,8,2,96]{3,2,1,0:T(2,128)} reshape(f32[96,1536]{1,0:T(8,128)} %get-tuple-element.6) | data formatting | bytes 1179648 | tf_op jit(solution)/shard_map/squeeze | solution.py:41
  44.8 3.1 %fusion.45 = (f32[96,8,1,96]{3,2,1,0:T(1,128)}, f32[96,8,1,96]{3,2,1,0:T(1,128)}) fusion(f32[96,8,2,96]{3,2,1,0:T(2,128)} %squeeze.7), kind=kLoop, calls=%fused_computation.114 | loop fusion | bytes 1179648 | tf_op jit(solution)/shard_map/slice | solution.py:43
  47.9 4.2 %copy.87 = f32[96,8,1,96]{1,3,0,2:T(8,128)} copy(f32[96,8,1,96]{3,2,1,0:T(1,128)} %get-tuple-element.10) | data formatting | bytes 589824
  52.1 3.0 %squeeze.8 = f32[96,8,2,96]{3,2,1,0:T(2,128)} reshape(f32[96,1536]{1,0:T(8,128)} %get-tuple-element.5) | data formatting | bytes 1179648 | tf_op jit(solution)/shard_map/squeeze | solution.py:42
  55.1 2.9 %fusion.44 = (f32[96,8,1,96]{3,2,1,0:T(1,128)}, f32[96,8,1,96]{3,2,1,0:T(1,128)}) fusion(f32[96,8,2,96]{3,2,1,0:T(2,128)} %squeeze.8), kind=kLoop, calls=%fused_computation.113 | loop fusion | bytes 1179648 | tf_op jit(solution)/shard_map/slice | solution.py:43
  58.0 4.2 %copy.88 = f32[96,8,1,96]{1,3,0,2:T(8,128)} copy(f32[96,8,1,96]{3,2,1,0:T(1,128)} %get-tuple-element.8) | data formatting | bytes 589824
  62.2 6.9 %sub.9 = f32[96,8,1,96]{1,3,0,2:T(8,128)} subtract(f32[96,8,1,96]{1,3,0,2:T(8,128)} %copy.87, f32[96,8,1,96]{1,3,0,2:T(8,128)} %copy.88) | non-fusion elementwise | flops 73728 | bytes 884736 | tf_op jit(solution)/shard_map/sub | solution.py:44
  69.1 6.2 %copy.73 = f32[48,2,8,1,48,2]{4,2,5,3,1,0:T(8,128)} copy(f32[48,2,8,1,48,2]{2,5,4,1,0,3:T(2,128)} %bitcast.147) | data formatting | bytes 589824 | tf_op jit(solution)/shard_map/stack | solution.py:45
  75.3 4.2 %copy.85 = f32[96,8,1,96]{1,3,0,2:T(8,128)} copy(f32[96,8,1,96]{3,2,1,0:T(1,128)} %get-tuple-element.9) | data formatting | bytes 589824
  79.5 4.2 %copy.86 = f32[96,8,1,96]{1,3,0,2:T(8,128)} copy(f32[96,8,1,96]{3,2,1,0:T(1,128)} %get-tuple-element.7) | data formatting | bytes 589824
  83.7 6.9 %add.60 = f32[96,8,1,96]{1,3,0,2:T(8,128)} add(f32[96,8,1,96]{1,3,0,2:T(8,128)} %copy.85, f32[96,8,1,96]{1,3,0,2:T(8,128)} %copy.86) | non-fusion elementwise | flops 73728 | bytes 884736 | tf_op jit(solution)/shard_map/add | solution.py:43
  90.6 6.2 %copy.72 = f32[48,2,8,1,48,2]{4,2,5,3,1,0:T(8,128)} copy(f32[48,2,8,1,48,2]{2,5,4,1,0,3:T(2,128)} %bitcast.148) | data formatting | bytes 589824 | tf_op jit(solution)/shard_map/stack | solution.py:45
  99.8 2.6 reshape.121
  116.2 16.9 %all_to_all.50 = bf16[16,8,2,2,2,144]{5,1,4,3,2,0:T(8,128)(2,1)S(1)} all-to-all(bf16[16,8,2,2,2,144]{5,1,4,3,2,0:T(8,128)(2,1)S(1)} %constant_dynamic-update-slice_fusion), channel_id=1, replica_groups=mesh['batch'=2,'rows'=16] {'rows'}, dimensions={0} | all-to-all | bytes 589824 | tf_op jit(solution)/shard_map/all_to_all | solution.py:125
  140.2 4.0 %fusion.48 = f32[144,64,128]{2,1,0:T(8,128)} fusion(bf16[144,64,8]{1,2,0:T(8,128)(2,1)} %bitcast.157, bf16[144,128,8]{1,2,0:T(8,128)(2,1)} %bitcast.152), kind=kOutput, calls=%fused_computation.117 | convolution fusion | flops 18874368 | bytes 5160960 | tf_op jit(solution)/shard_map/bik,bxk->bix/dot_general | solution.py:137
  144.3 3.0 %convolution_convert_fusion = bf16[144,8,64]{2,1,0:T(8,128)(2,1)} fusion(bf16[144,128,8]{1,2,0:T(8,128)(2,1)} %bitcast.153, bf16[144,64,128]{2,1,0:T(8,128)(2,1)S(1)} %copy-done), kind=kOutput, calls=%fused_computation.26 | convolution fusion | flops 18948096 | bytes 2801664 | tf_op jit(solution)/shard_map/bix,bxk->bik/dot_general | solution.py:134
  147.3 2.0 copy.77
  149.3 4.4 %all-to-all-start.2 = ((bf16[64,2,2,2,144]{4,3,2,1,0:T(2,128)(2,1)}), bf16[64,2,2,2,144]{4,3,2,1,0:T(2,128)(2,1)}, u32[]{:S(2)}, u32[]{:S(2)}) async-start(bf16[64,2,2,2,144]{4,3,2,1,0:T(2,128)(2,1)} %bitcast.158), calls=%async_computation.2 | async-start | bytes 524288 | tf_op jit(solution)/shard_map/all_to_all | solution.py:141
  155.4 42.3 %psum.15 = f32[64,64]{1,0:T(8,128)} all-reduce(f32[64,64]{1,0:T(8,128)S(1)} %convolution_bitcast_fusion.1), channel_id=1, replica_groups=mesh['batch'=2,'rows'=16] {'batch','rows'}, use_global_device_ids=true, to_apply=%region_1.2 | all-reduce | flops 4096 | bytes 32768 | tf_op jit(solution)/shard_map/psum | solution.py:158
  199.5 2.1 reshape.124
  201.6 13.9 %copy.80 = bf16[48,2,4,2,48,2]{2,5,4,3,1,0:T(2,128)(2,1)} copy(bf16[48,2,4,2,48,2]{4,0,5,1,3,2:T(8,128)(2,1)} %bitcast.150) | data formatting | bytes 294912 | tf_op jit(solution)/shard_map/transpose | solution.py:57
  215.5 8.4 %copy.79 = bf16[48,2,4,2,48,2]{5,4,3,2,1,0:T(8,128)(2,1)} copy(bf16[48,2,4,2,48,2]{4,0,5,1,3,2:T(8,128)(2,1)} %bitcast.151) | data formatting | bytes 294912 | tf_op jit(solution)/shard_map/transpose | solution.py:57
  223.9 2.9 %slice_negate_fusion = (bf16[96,4,1,96]{1,3,2,0:T(8,128)(2,1)S(1)}, bf16[96,4,1,96]{1,3,2,0:T(8,128)(2,1)S(1)}) fusion(bf16[96,4,2,96]{1,3,2,0:T(8,128)(2,1)} %bitcast.149), kind=kLoop, calls=%fused_computation.10 | loop fusion | flops 36864 | bytes 294912 | tf_op jit(solution)/shard_map/neg | solution.py:83
  226.8 3.1 %pad_maximum_fusion = bf16[96,4,2,96]{1,3,2,0:T(8,128)(2,1)} fusion(bf16[96,4,1,96]{1,3,2,0:T(8,128)(2,1)S(1)} %get-tuple-element.4, bf16[96,4,1,96]{1,3,2,0:T(8,128)(2,1)S(1)} %get-tuple-element.3), kind=kLoop, calls=%fused_computation | loop fusion | flops 73728 | bytes 294912 | tf_op jit(solution)/shard_map/stack | solution.py:83
  229.9 4.8 %copy.81 = bf16[96,4,2,96]{3,2,1,0:T(2,128)(2,1)} copy(bf16[96,4,2,96]{1,3,2,0:T(8,128)(2,1)} %pad_maximum_fusion) | data formatting | bytes 294912 | tf_op jit(solution)/shard_map/stack | solution.py:83
  235.8 17.1 %concatenate.27 = bf16[96,768]{1,0:T(8,128)(2,1)} reshape(bf16[48,2,4,2,48,2]{5,4,3,2,1,0:T(8,128)(2,1)} %copy.79) | data formatting | bytes 294912 | tf_op jit(solution)/shard_map/concatenate | solution.py:84
  256.4 5.4 %all-to-all-start.3 = ((bf16[64,4,192]{2,1,0:T(4,128)(2,1)}), bf16[64,4,192]{2,1,0:T(4,128)(2,1)S(1)}, u32[]{:S(2)}, u32[]{:S(2)}) async-start(bf16[64,4,192]{2,1,0:T(4,128)(2,1)} %reshape.126), calls=%async_computation.3 | async-start | bytes 262144 | tf_op jit(solution)/shard_map/all_to_all | solution.py:146
  263.2 6.5 %all-to-all-done.3 = bf16[64,4,192]{2,1,0:T(4,128)(2,1)S(1)} async-done(((bf16[64,4,192]{2,1,0:T(4,128)(2,1)}), bf16[64,4,192]{2,1,0:T(4,128)(2,1)S(1)}, u32[]{:S(2)}, u32[]{:S(2)}) %all-to-all-start.3) | async-done | bytes 98336 | tf_op jit(solution)/shard_map/all_to_all | solution.py:146
  274.4 5.2 %copy.113 = f32[144,64,128]{2,1,0:T(8,128)} copy(f32[144,64,128]{2,1,0:T(8,128)} %all-reduce.2.cloned.1.call-done) | data formatting | bytes 9437184
  (81 shorter events, 51.9 us)
Async XLA Ops:
  7.2 137.1 %copy-start = (bf16[144,64,128]{2,1,0:T(8,128)(2,1)S(1)}, bf16[144,64,128]{2,1,0:T(8,128)(2,1)}, u32[]{:S(2)}) copy-start(bf16[144,64,128]{2,1,0:T(8,128)(2,1)} %param.11) | copy-start | bytes 7077892
  11.9 1.6 copy-start.4
  11.9 1.9 copy-start.5
  12.0 2.9 %copy-start.6 = (f32[4,2048]{1,0:T(4,128)}, f32[4,2048]{1,0:T(4,128)S(1)}, u32[]{:S(2)}) copy-start(f32[4,2048]{1,0:T(4,128)S(1)} %get-tuple-element.18) | copy-start | bytes 98308
  13.5 1.4 copy-start.1
  13.5 1.4 copy-start.2
  13.5 1.6 copy-start.3
  15.1 11.1 %copy-start.11 = (s32[1,32]{1,0:T(1,128)S(1)}, s32[1,32]{1,0:T(1,128)}, u32[]{:S(2)}) copy-start(s32[1,32]{1,0:T(1,128)} %param.12) | copy-start | bytes 388
  18.4 17.5 %all-to-all-start = ((bf16[4,128,192]{2,0,1:T(4,128)(2,1)}), bf16[4,128,192]{2,0,1:T(4,128)(2,1)}, u32[]{:S(2)}, u32[]{:S(2)}) async-start(bf16[4,128,192]{2,0,1:T(4,128)(2,1)} %copy.65), calls=%async_computation | async-start | bytes 524288 | tf_op jit(solution)/shard_map/all_to_all | solution.py:116
  25.9 248.5 %all-reduce.2.cloned.1.call-start = ((), (), s32[]{:S(2)}) async-start(), calls=%async_computation.4 | async-start | bytes 9437184 | tf_op jit(solution)/shard_map/psum | solution.py:140
  26.6 15.2 %copy-start.8 = (bf16[96,64]{1,0:T(8,128)(2,1)}, bf16[96,64]{1,0:T(8,128)(2,1)S(1)}, u32[]{:S(2)}) copy-start(bf16[96,64]{1,0:T(8,128)(2,1)S(1)} %get-tuple-element.15) | copy-start | bytes 36868
  26.6 15.2 %copy-start.9 = (bf16[96,64]{1,0:T(8,128)(2,1)}, bf16[96,64]{1,0:T(8,128)(2,1)S(1)}, u32[]{:S(2)}) copy-start(bf16[96,64]{1,0:T(8,128)(2,1)S(1)} %get-tuple-element.16) | copy-start | bytes 36868
  149.3 48.4 %all-to-all-start.2 = ((bf16[64,2,2,2,144]{4,3,2,1,0:T(2,128)(2,1)}), bf16[64,2,2,2,144]{4,3,2,1,0:T(2,128)(2,1)}, u32[]{:S(2)}, u32[]{:S(2)}) async-start(bf16[64,2,2,2,144]{4,3,2,1,0:T(2,128)(2,1)} %bitcast.158), calls=%async_computation.2 | async-start | bytes 524288 | tf_op jit(solution)/shard_map/all_to_all | solution.py:141
  254.7 18.3 %copy-start.10 = (bf16[64,64]{1,0:T(8,128)(2,1)S(1)}, bf16[64,64]{1,0:T(8,128)(2,1)}, u32[]{:S(2)}) copy-start(bf16[64,64]{1,0:T(8,128)(2,1)} %param.10) | copy-start | bytes 24580
  256.4 13.3 %all-to-all-start.3 = ((bf16[64,4,192]{2,1,0:T(4,128)(2,1)}), bf16[64,4,192]{2,1,0:T(4,128)(2,1)S(1)}, u32[]{:S(2)}, u32[]{:S(2)}) async-start(bf16[64,4,192]{2,1,0:T(4,128)(2,1)} %reshape.126), calls=%async_computation.3 | async-start | bytes 262144 | tf_op jit(solution)/shard_map/all_to_all | solution.py:146
  271.4 1.6 copy-start.7
Sparse Core Ops, SparseCore 0:
  144.4 120.1 all-reduce.1
